TPU v7x, 256 devices: a whole 4x4x8 slice. The times are simulated.
256 devices in a mesh: cell: 64 (over x, z_hi, y, core), cls: 4 (over z_lo).
Axes of the slice: x: 4, y: 4, z: 8 (z_hi: 2, z_lo: 4; z = z_hi * 4 + z_lo), core: 2. Of those that a mesh axis runs over, the one named last changes fastest.
Arguments:
- melt: float32 [64, 32, 65536], P(None, 'cls', 'cell'), may hold values from 0 to 1
- counts: int32 [32, 65536], P('cls', 'cell'), may hold values from 0 to 800, as said below
- pressure: float32 [256, 256], P(('cell', 'cls')), may hold values from 0.5 to 2
- propagator: float32 [32, 64, 64], replicated, as said below
- coupling: float32 [32, 64], replicated, may hold values from 0.05 to 0.5
- flux_weights: float32 [32, 64], replicated, may hold values from 0.002 to 0.2
Outputs:
- shells_out: float32 [64, 32, 65536], P(None, 'cls', 'cell')
- pressure_out: float32 [256, 256], P(('cell', 'cls'))
Inputs may be any that keep to these rules, and one draw needn't show every extreme that they name: counts in layer l are non-negative and below 201 + (600 * l) // 255. Each propagator matrix has a dominant diagonal.
All inputs are finite; a program needn't handle non-finite values.
Results may differ from a plain program's by a relative error of at most 0.0001.
Values sent between devices are 32-bit elements; how exact they have to be, the bound alone decides.
A program may use at most 64 MiB of HBM per device.

v0:
```python
import jax
import jax.numpy as jnp
from jax import lax
from jax.sharding import PartitionSpec as P

CLASSES = 32
SIDE = 16
SUBSTEPS = 4
count_scale = 400.0


def extended_2(block, sides, width):
    for axis, dim in sides:
        count = lax.axis_size(axis)
        forward = [(i, i + 1) for i in range(count - 1)]
        backward = [(target, source) for source, target in forward]
        low = lax.ppermute(
            lax.slice_in_dim(block, block.shape[dim] - width, None, axis=dim), axis, forward
        )
        high = lax.ppermute(lax.slice_in_dim(block, 0, width, axis=dim), axis, backward)
        block = jnp.concatenate([low, block, high], axis=dim)
    return block


def shell_update(shells, counts_f, propagator, coupling, flux_weights, wall):
    shells = (
        jnp.einsum("kij,jkc->ikc", propagator, shells, precision=lax.Precision.HIGHEST)
        + coupling.T[:, :, None] * wall[None, None, :]
    )
    flux = jnp.einsum("ki,ikc->kc", flux_weights, shells, precision=lax.Precision.HIGHEST)
    partial_gas = jnp.sum(counts_f * flux, axis=0) / (count_scale * CLASSES)
    return (shells, partial_gas)


def pressure_update(tile, gas_tile):
    total = lax.psum(jnp.sum(gas_tile), ("cell", "cls"))
    all_cells = gas_tile.shape[0] * lax.axis_size("cell") * lax.axis_size("cls")
    chamber = 1.5 - 0.5 * total / all_cells
    layer_count = tile.shape[0]
    field = tile.reshape(layer_count, SIDE, SIDE)
    extended = extended_2(field, ((("cell", "cls"), 0),), 1)
    extended = jnp.pad(extended, ((0, 0), (1, 1), (1, 1)))
    lap = (
        extended[2:, 1:-1, 1:-1]
        + extended[:-2, 1:-1, 1:-1]
        + extended[1:-1, 2:, 1:-1]
        + extended[1:-1, :-2, 1:-1]
        + extended[1:-1, 1:-1, 2:]
        + extended[1:-1, 1:-1, :-2]
        - 6.0 * field
    )
    field = field + 0.15 * lap + 0.1 * gas_tile.reshape(field.shape) + 0.2 * (chamber - field)
    return field.reshape(tile.shape)


def shards(melt, counts, pressure, propagator, coupling, flux_weights):
    tile = pressure
    class_count = melt.shape[1]
    start = lax.axis_index("cls") * class_count
    local_prop = lax.dynamic_slice_in_dim(propagator, start, class_count, 0)
    local_coupling = lax.dynamic_slice_in_dim(coupling, start, class_count, 0)
    local_flux = lax.dynamic_slice_in_dim(flux_weights, start, class_count, 0)
    counts_f = counts.astype(jnp.float32)
    shells = melt
    for step in range(SUBSTEPS):
        block_pressure = lax.all_gather(tile.reshape(-1), "cls", axis=0, tiled=True)
        shells, partial_gas = shell_update(
            shells, counts_f, local_prop, local_coupling, local_flux, 0.5 * block_pressure
        )
        gas_tile = lax.psum_scatter(partial_gas, "cls", scatter_dimension=0, tiled=True)
        tile = pressure_update(tile, gas_tile)
    return (shells, tile)


def solution(mesh):
    placed = (P(None, "cls", "cell"), P("cls", "cell"), P(("cell", "cls"), None), P(), P(), P())
    return jax.shard_map(
        shards,
        mesh=mesh,
        in_specs=placed,
        out_specs=(P(None, "cls", "cell"), P(("cell", "cls"), None)),
        check_vma=False,
    )
```

profile of v0, /device:TPU:1, one launch (start us, length us, event | category | flops | bytes accessed | tf_op | source)
XLA Modules:
  0.0 445.1 jit_solution(3294544564548670002)
XLA Ops:
  1.2 1.5 reduce.3
  2.7 4.4 collective-permute-start.1
  7.1 5.2 %collective-permute-start = (f32[1,16,16]{2,1,0:T(8,128)S(1)}, f32[1,16,16]{2,1,0:T(8,128)S(1)}, u32[]{:S(2)}, u32[]{:S(2)}) collective-permute-start(f32[1,16,16]{2,1,0:T(8,128)S(1)} %reshape.107), channel_id=1, source_target_pairs={{1,0},{2,1},{3,2},{4,3},{5,4},{6,5},{7,6},{8,7},{9,8},{10,9},{11,1... | collective-permute-start | bytes 3080 | tf_op jit(solution)/shard_map/ppermute | solution.py:20
  12.3 7.0 %all-gather = f32[1,1024]{1,0:T(1,128)S(1)} all-gather(f32[1,256]{1,0:T(1,128)} %param.8), channel_id=2, replica_groups=mesh['cell'=64,'cls'=4] {'cls'}, dimensions={1}, use_global_device_ids=true | all-gather | bytes 5120 | tf_op jit(solution)/shard_map/all_gather | solution.py:66
  19.2 1.3 dynamic-slice
  21.9 4.0 fusion
  25.9 1.3 copy-done.1
  27.2 1.3 fusion.2
  28.6 7.5 %all-reduce.4 = f32[1024]{0:T(1024)S(1)} all-reduce(f32[1024]{0:T(1024)S(1)} %broadcast_multiply_fusion.7), channel_id=3, replica_groups=mesh['cell'=64,'cls'=4] {'cls'}, use_global_device_ids=true, to_apply=%region_1.0.clone | all-reduce | flops 1024 | bytes 8192
  36.7 80.6 %psum.28 = f32[]{:T(128)} all-reduce(f32[]{:T(128)} %get-tuple-element.12), channel_id=1, replica_groups=mesh['cell'=64,'cls'=4] {'cell','cls'}, use_global_device_ids=true, to_apply=%region_3.0 | all-reduce | flops 1 | bytes 8 | tf_op jit(solution)/shard_map/psum | solution.py:36
  118.3 3.5 collective-permute-start.3
  121.8 4.4 collective-permute-start.2
  126.2 6.7 %all-gather.1 = f32[4,1,256]{2,1,0:T(1,128)S(1)} all-gather(f32[1,1,256]{2,1,0:T(1,128)S(1)} %reshape.112), channel_id=1, replica_groups=mesh['cell'=64,'cls'=4] {'cls'}, dimensions={0}, use_global_device_ids=true | all-gather | bytes 5120 | tf_op jit(solution)/shard_map/all_gather | solution.py:66
  132.9 3.9 bitcast_add_fusion.2
  136.9 1.1 fusion.50
  138.0 3.3 fusion.15
  141.3 7.5 %all-reduce.5 = f32[1024]{0:T(1024)S(1)} all-reduce(f32[1024]{0:T(1024)S(1)} %broadcast_multiply_fusion.6), channel_id=4, replica_groups=mesh['cell'=64,'cls'=4] {'cls'}, use_global_device_ids=true, to_apply=%region_5.6.clone | all-reduce | flops 1024 | bytes 8192
  149.5 78.4 %psum.29 = f32[]{:T(128)} all-reduce(f32[]{:T(128)} %get-tuple-element.10), channel_id=1, replica_groups=mesh['cell'=64,'cls'=4] {'cell','cls'}, use_global_device_ids=true, to_apply=%region_7.8 | all-reduce | flops 1 | bytes 8 | tf_op jit(solution)/shard_map/psum | solution.py:36
  228.9 3.7 collective-permute-start.5
  232.6 3.8 collective-permute-start.4
  236.4 6.5 %all-gather.2 = f32[4,1,256]{2,1,0:T(1,128)S(1)} all-gather(f32[1,1,256]{2,1,0:T(1,128)S(1)} %reshape.114), channel_id=1, replica_groups=mesh['cell'=64,'cls'=4] {'cls'}, dimensions={0}, use_global_device_ids=true | all-gather | bytes 5120 | tf_op jit(solution)/shard_map/all_gather | solution.py:66
  242.8 2.9 fusion.4
  245.8 7.8 %all-reduce.6 = f32[1024]{0:T(1024)S(1)} all-reduce(f32[1024]{0:T(1024)S(1)} %broadcast_multiply_fusion.5), channel_id=5, replica_groups=mesh['cell'=64,'cls'=4] {'cls'}, use_global_device_ids=true, to_apply=%region_9.10.clone | all-reduce | flops 1024 | bytes 8192
  254.2 77.2 %psum.30 = f32[]{:T(128)} all-reduce(f32[]{:T(128)} %get-tuple-element.8), channel_id=1, replica_groups=mesh['cell'=64,'cls'=4] {'cell','cls'}, use_global_device_ids=true, to_apply=%region_11.12 | all-reduce | flops 1 | bytes 8 | tf_op jit(solution)/shard_map/psum | solution.py:36
  332.4 3.7 collective-permute-start.7
  336.1 3.7 collective-permute-start.6
  339.8 6.1 %all-gather.3 = f32[4,1,256]{2,1,0:T(1,128)S(1)} all-gather(f32[1,1,256]{2,1,0:T(1,128)S(1)} %reshape.116), channel_id=1, replica_groups=mesh['cell'=64,'cls'=4] {'cls'}, dimensions={0}, use_global_device_ids=true | all-gather | bytes 5120 | tf_op jit(solution)/shard_map/all_gather | solution.py:66
  345.9 3.9 bitcast_add_fusion
  349.9 1.3 copy-done.2
  352.3 8.0 %all-reduce.7 = f32[1024]{0:T(1024)S(1)} all-reduce(f32[1024]{0:T(1024)S(1)} %broadcast_multiply_fusion.4), channel_id=6, replica_groups=mesh['cell'=64,'cls'=4] {'cls'}, use_global_device_ids=true, to_apply=%region_13.14.clone | all-reduce | flops 1024 | bytes 8192
  361.0 78.4 %psum.31 = f32[]{:T(128)} all-reduce(f32[]{:T(128)} %get-tuple-element.6), channel_id=1, replica_groups=mesh['cell'=64,'cls'=4] {'cell','cls'}, use_global_device_ids=true, to_apply=%region_15.16 | all-reduce | flops 1 | bytes 8 | tf_op jit(solution)/shard_map/psum | solution.py:36
  439.4 4.1 copy.11
  (52 shorter events, 7.1 us)
Async XLA Ops:
  0.6 21.2 %copy-start = (f32[64,8,1024]{2,1,0:T(8,128)S(1)}, f32[64,8,1024]{2,1,0:T(8,128)}, u32[]{:S(2)}) copy-start(f32[64,8,1024]{2,1,0:T(8,128)} %param.6) | copy-start | bytes 6291460
  2.7 115.4 %collective-permute-start.1 = (f32[1,16,16]{2,1,0:T(8,128)S(1)}, f32[1,16,16]{2,1,0:T(8,128)S(1)}, u32[]{:S(2)}, u32[]{:S(2)}) collective-permute-start(f32[1,16,16]{2,1,0:T(8,128)S(1)} %reshape.107), channel_id=1, source_target_pairs={{0,1},{1,2},{2,3},{3,4},{4,5},{5,6},{6,7},{7,8},{8,9},{9,10},{10,1... | collective-permute-start | bytes 3080 | tf_op jit(solution)/shard_map/ppermute | solution.py:17
  7.1 111.0 %collective-permute-start = (f32[1,16,16]{2,1,0:T(8,128)S(1)}, f32[1,16,16]{2,1,0:T(8,128)S(1)}, u32[]{:S(2)}, u32[]{:S(2)}) collective-permute-start(f32[1,16,16]{2,1,0:T(8,128)S(1)} %reshape.107), channel_id=1, source_target_pairs={{1,0},{2,1},{3,2},{4,3},{5,4},{6,5},{7,6},{8,7},{9,8},{10,9},{11,1... | collective-permute-start | bytes 3080 | tf_op jit(solution)/shard_map/ppermute | solution.py:20
  25.9 1.3 copy-start.1
  25.9 2.6 copy-start.4
  25.9 107.0 %copy-start.3 = (f32[32,64,64]{2,1,0:T(8,128)S(1)}, f32[32,64,64]{2,1,0:T(8,128)}, u32[]{:S(2)}) copy-start(f32[32,64,64]{2,1,0:T(8,128)} %param.9) | copy-start | bytes 1572868
  118.3 110.3 %collective-permute-start.3 = (f32[1,16,16]{2,1,0:T(8,128)S(1)}, f32[1,16,16]{2,1,0:T(8,128)S(1)}, u32[]{:S(2)}, u32[]{:S(2)}) collective-permute-start(f32[1,16,16]{2,1,0:T(8,128)S(1)} %fusion.45), channel_id=1, source_target_pairs={{0,1},{1,2},{2,3},{3,4},{4,5},{5,6},{6,7},{7,8},{8,9},{9,10},{10,1... | collective-permute-start | bytes 3080 | tf_op jit(solution)/shard_map/ppermute | solution.py:17
  121.8 106.8 %collective-permute-start.2 = (f32[1,16,16]{2,1,0:T(8,128)S(1)}, f32[1,16,16]{2,1,0:T(8,128)S(1)}, u32[]{:S(2)}, u32[]{:S(2)}) collective-permute-start(f32[1,16,16]{2,1,0:T(8,128)S(1)} %fusion.45), channel_id=1, source_target_pairs={{1,0},{2,1},{3,2},{4,3},{5,4},{6,5},{7,6},{8,7},{9,8},{10,9},{11,1... | collective-permute-start | bytes 3080 | tf_op jit(solution)/shard_map/ppermute | solution.py:20
  228.9 103.3 %collective-permute-start.5 = (f32[1,16,16]{2,1,0:T(8,128)S(1)}, f32[1,16,16]{2,1,0:T(8,128)S(1)}, u32[]{:S(2)}, u32[]{:S(2)}) collective-permute-start(f32[1,16,16]{2,1,0:T(8,128)S(1)} %fusion.40), channel_id=1, source_target_pairs={{0,1},{1,2},{2,3},{3,4},{4,5},{5,6},{6,7},{7,8},{8,9},{9,10},{10,1... | collective-permute-start | bytes 3080 | tf_op jit(solution)/shard_map/ppermute | solution.py:17
  232.6 99.6 %collective-permute-start.4 = (f32[1,16,16]{2,1,0:T(8,128)S(1)}, f32[1,16,16]{2,1,0:T(8,128)S(1)}, u32[]{:S(2)}, u32[]{:S(2)}) collective-permute-start(f32[1,16,16]{2,1,0:T(8,128)S(1)} %fusion.40), channel_id=1, source_target_pairs={{1,0},{2,1},{3,2},{4,3},{5,4},{6,5},{7,6},{8,7},{9,8},{10,9},{11,1... | collective-permute-start | bytes 3080 | tf_op jit(solution)/shard_map/ppermute | solution.py:20
  332.4 111.8 %collective-permute-start.7 = (f32[1,16,16]{2,1,0:T(8,128)S(1)}, f32[1,16,16]{2,1,0:T(8,128)S(1)}, u32[]{:S(2)}, u32[]{:S(2)}) collective-permute-start(f32[1,16,16]{2,1,0:T(8,128)S(1)} %fusion.35), channel_id=1, source_target_pairs={{0,1},{1,2},{2,3},{3,4},{4,5},{5,6},{6,7},{7,8},{8,9},{9,10},{10,1... | collective-permute-start | bytes 3080 | tf_op jit(solution)/shard_map/ppermute | solution.py:17
  336.1 108.2 %collective-permute-start.6 = (f32[1,16,16]{2,1,0:T(8,128)S(1)}, f32[1,16,16]{2,1,0:T(8,128)S(1)}, u32[]{:S(2)}, u32[]{:S(2)}) collective-permute-start(f32[1,16,16]{2,1,0:T(8,128)S(1)} %fusion.35), channel_id=1, source_target_pairs={{1,0},{2,1},{3,2},{4,3},{5,4},{6,5},{7,6},{8,7},{9,8},{10,9},{11,1... | collective-permute-start | bytes 3080 | tf_op jit(solution)/shard_map/ppermute | solution.py:20
  349.9 1.4 copy-start.2
where the time goes:
time: 446 us; the launch traced here: 445 us
  blocking collectives  372 us (83%)
  starting transfers between devices  32.2 us (7%)
  matrix products  21.6 us (5%)
  local copies, waits for them, and re-layouts  10.6 us (2%)
  other arithmetic  4.92 us (1%)
    psum x4, blocking collectives, pressure_update(): total = lax.psum(jnp.sum(gas_tile), ('cell', 'cls'))  315 us
    unnamed x4, blocking collectives  30.7 us
    all_gather x4, blocking collectives, shards(): block_pressure = lax.all_gather(tile.reshape(-1), 'cls', axis=0, tiled=True)  26.3 us
    ppermute x4, starting transfers between devices, extended_2(): lax.ppermute(lax.slice_in_dim(block, 0, width, axis=dim), axis, backward)  17 us
    ppermute x4, starting transfers between devices, extended_2(): lax.ppermute(lax.slice_in_dim(block, block.shape[dim] - width, None, axis...  15.2 us
    dot_general x4, matrix products, shell_update(): jnp.einsum('kij,jkc->ikc', propagator, shells, precision=lax.Precision.HI...  15.2 us
  transfers between devices with their start and end apart: 8, of which 0 were waited for; matrix products, arithmetic and copies ran while one was open for 7% of the time, Pallas kernels for 0%

commit v1 on v0

--- a/solution.py
+++ b/solution.py
@@ -63,7 +63,10 @@
     counts_f = counts.astype(jnp.float32)
     shells = melt
     for step in range(SUBSTEPS):
-        block_pressure = lax.all_gather(tile.reshape(-1), "cls", axis=0, tiled=True)
+        block_pressure = jnp.concatenate(
+            lax.all_to_all(jnp.stack([tile.reshape(-1)] * lax.axis_size("cls")), "cls", 0, 0),
+            axis=0,
+        )
         shells, partial_gas = shell_update(
             shells, counts_f, local_prop, local_coupling, local_flux, 0.5 * block_pressure
         )

time: 446 us -> 449 us (level)
  blocking collectives: 372 us -> 344 us
  starting transfers between devices: 32.2 us -> 45.5 us
  waiting for transfers between devices: 0.02 us -> 12.9 us
    all_gather x4 -> x0, blocking collectives: 26.3 us -> none  [shards(): block_pressure = lax.all_gather(tile.reshape(-1), 'cls', axis=0, tiled=True)]
    all_to_all x0 -> x4, starting transfers between devices: none -> 13 us  [shards(): lax.all_to_all(jnp.stack([tile.reshape(-1)] * lax.axis_size('cls')), 'cls...]
    all_to_all x0 -> x4, waiting for transfers between devices: none -> 12.9 us  [shards(): lax.all_to_all(jnp.stack([tile.reshape(-1)] * lax.axis_size('cls')), 'cls...]
  transfers between devices with their start and end apart: 8 -> 12, of which waited for: 0 -> 3; matrix products, arithmetic and copies ran while one was open for 7% -> 3% of each run, Pallas kernels for 0% -> 0%
where the time goes in v1:
time: 449 us; the launch traced here: 447 us
  blocking collectives  344 us (77%)
  starting transfers between devices  45.5 us (10%)
  matrix products  26 us (6%)
  waiting for transfers between devices  12.9 us (3%)
  local copies, waits for them, and re-layouts  10.1 us (2%)
  other arithmetic  4.92 us (1%)
    psum x4, blocking collectives, pressure_update(): total = lax.psum(jnp.sum(gas_tile), ('cell', 'cls'))  312 us
    unnamed x4, blocking collectives  31.7 us
    ppermute x4, starting transfers between devices, extended_2(): lax.ppermute(lax.slice_in_dim(block, 0, width, axis=dim), axis, backward)  18.2 us
    dot_general x4, matrix products, shell_update(): jnp.einsum('kij,jkc->ikc', propagator, shells, precision=lax.Precision.HI...  18 us
    ppermute x4, starting transfers between devices, extended_2(): lax.ppermute(lax.slice_in_dim(block, block.shape[dim] - width, None, axis...  14.3 us
    all_to_all x4, starting transfers between devices, shards(): lax.all_to_all(jnp.stack([tile.reshape(-1)] * lax.axis_size('cls')), 'cls...  13 us
    all_to_all x4, waiting for transfers between devices, shards(): lax.all_to_all(jnp.stack([tile.reshape(-1)] * lax.axis_size('cls')), 'cls...  12.9 us
  transfers between devices with their start and end apart: 12, of which 3 were waited for; matrix products, arithmetic and copies ran while one was open for 3% of the time, Pallas kernels for 0%

profile of v1, /device:TPU:1, one launch (start us, length us, event | category | flops | bytes accessed | tf_op | source)
XLA Modules:
  0.0 447.2 jit_solution(18333821294041551090)
XLA Ops:
  1.2 1.5 reduce.3
  2.7 4.4 collective-permute-start.1
  7.1 5.2 %collective-permute-start = (f32[1,16,16]{2,1,0:T(8,128)S(1)}, f32[1,16,16]{2,1,0:T(8,128)S(1)}, u32[]{:S(2)}, u32[]{:S(2)}) collective-permute-start(f32[1,16,16]{2,1,0:T(8,128)S(1)} %reshape.169), channel_id=1, source_target_pairs={{1,0},{2,1},{3,2},{4,3},{5,4},{6,5},{7,6},{8,7},{9,8},{10,9},{11,1... | collective-permute-start | bytes 3080 | tf_op jit(solution)/shard_map/ppermute | solution.py:20
  13.5 3.2 all-to-all-start
  16.8 5.3 %fusion = f32[8,64,1024]{2,1,0:T(8,128)} fusion(f32[64,8,1024]{2,1,0:T(8,128)S(1)} %copy-done, f32[32,64,64]{2,1,0:T(8,128)} %param.9, s32[]{:T(128)S(6)} %select_n.2), kind=kOutput, calls=%fused_computation.4 | convolution fusion | flops 402653184 | bytes 4456452 | tf_op jit(solution)/shard_map/kij,jkc->ikc/dot_general | solution.py:27
  24.3 2.9 fusion.2
  27.2 9.9 %all-reduce.4 = f32[1024]{0:T(1024)S(1)} all-reduce(f32[1024]{0:T(1024)S(1)} %broadcast_multiply_fusion.3), channel_id=2, replica_groups=mesh['cell'=64,'cls'=4] {'cls'}, use_global_device_ids=true, to_apply=%region_1.0.clone | all-reduce | flops 1024 | bytes 8192
  37.8 78.9 %psum.28 = f32[]{:T(128)} all-reduce(f32[]{:T(128)} %get-tuple-element.12), channel_id=1, replica_groups=mesh['cell'=64,'cls'=4] {'cell','cls'}, use_global_device_ids=true, to_apply=%region_3.0 | all-reduce | flops 1 | bytes 8 | tf_op jit(solution)/shard_map/psum | solution.py:36
  117.5 3.7 collective-permute-start.3
  121.2 4.4 collective-permute-start.2
  126.2 3.2 all-to-all-start.1
  129.6 4.3 all-to-all-done.1
  133.9 3.9 bitcast_add_fusion.2
  137.8 1.3 copy-done.1
  140.3 7.2 %all-reduce.5 = f32[1024]{0:T(1024)S(1)} all-reduce(f32[1024]{0:T(1024)S(1)} %broadcast_multiply_fusion.2), channel_id=3, replica_groups=mesh['cell'=64,'cls'=4] {'cls'}, use_global_device_ids=true, to_apply=%region_5.6.clone | all-reduce | flops 1024 | bytes 8192
  148.2 78.1 %psum.29 = f32[]{:T(128)} all-reduce(f32[]{:T(128)} %get-tuple-element.10), channel_id=1, replica_groups=mesh['cell'=64,'cls'=4] {'cell','cls'}, use_global_device_ids=true, to_apply=%region_7.8 | all-reduce | flops 1 | bytes 8 | tf_op jit(solution)/shard_map/psum | solution.py:36
  227.1 2.7 collective-permute-start.5
  229.7 4.9 %collective-permute-start.4 = (f32[1,16,16]{2,1,0:T(8,128)S(1)}, f32[1,16,16]{2,1,0:T(8,128)S(1)}, u32[]{:S(2)}, u32[]{:S(2)}) collective-permute-start(f32[1,16,16]{2,1,0:T(8,128)S(1)} %fusion.40), channel_id=1, source_target_pairs={{1,0},{2,1},{3,2},{4,3},{5,4},{6,5},{7,6},{8,7},{9,8},{10,9},{11,1... | collective-permute-start | bytes 3080 | tf_op jit(solution)/shard_map/ppermute | solution.py:20
  234.6 4.9 %fusion.15 = f32[8,1024,64]{1,2,0:T(8,128)} fusion(f32[64,8,1024]{2,0,1:T(8,128)} %copy-done.1, f32[32,64,64]{2,1,0:T(8,128)S(1)} %copy-done.2, s32[]{:T(128)S(6)} %select_n.2), kind=kOutput, calls=%fused_computation.19 | convolution fusion | flops 402653184 | bytes 4456452 | tf_op jit(solution)/shard_map/kij,jkc->ikc/dot_general | solution.py:27
  240.2 3.2 all-to-all-start.2
  243.5 4.3 all-to-all-done.2
  247.8 2.9 fusion.4
  250.8 7.4 %all-reduce.6 = f32[1024]{0:T(1024)S(1)} all-reduce(f32[1024]{0:T(1024)S(1)} %broadcast_multiply_fusion.1), channel_id=4, replica_groups=mesh['cell'=64,'cls'=4] {'cls'}, use_global_device_ids=true, to_apply=%region_9.10.clone | all-reduce | flops 1024 | bytes 8192
  258.8 77.3 %psum.30 = f32[]{:T(128)} all-reduce(f32[]{:T(128)} %get-tuple-element.8), channel_id=1, replica_groups=mesh['cell'=64,'cls'=4] {'cell','cls'}, use_global_device_ids=true, to_apply=%region_11.12 | all-reduce | flops 1 | bytes 8 | tf_op jit(solution)/shard_map/psum | solution.py:36
  336.9 3.6 collective-permute-start.7
  340.6 3.7 collective-permute-start.6
  345.0 3.2 all-to-all-start.3
  348.3 4.3 all-to-all-done.3
  352.6 3.9 bitcast_add_fusion
  357.6 2.5 copy.11
  360.2 7.2 %all-reduce.7 = f32[1024]{0:T(1024)S(1)} all-reduce(f32[1024]{0:T(1024)S(1)} %broadcast_multiply_fusion), channel_id=5, replica_groups=mesh['cell'=64,'cls'=4] {'cls'}, use_global_device_ids=true, to_apply=%region_13.14.clone | all-reduce | flops 1024 | bytes 8192
  368.1 77.6 %psum.31 = f32[]{:T(128)} all-reduce(f32[]{:T(128)} %get-tuple-element.6), channel_id=1, replica_groups=mesh['cell'=64,'cls'=4] {'cell','cls'}, use_global_device_ids=true, to_apply=%region_15.16 | all-reduce | flops 1 | bytes 8 | tf_op jit(solution)/shard_map/psum | solution.py:36
  (60 shorter events, 12.0 us)
Async XLA Ops:
  0.6 16.2 %copy-start = (f32[64,8,1024]{2,1,0:T(8,128)S(1)}, f32[64,8,1024]{2,1,0:T(8,128)}, u32[]{:S(2)}) copy-start(f32[64,8,1024]{2,1,0:T(8,128)} %param.6) | copy-start | bytes 6291460
  2.7 21.5 %collective-permute-start.1 = (f32[1,16,16]{2,1,0:T(8,128)S(1)}, f32[1,16,16]{2,1,0:T(8,128)S(1)}, u32[]{:S(2)}, u32[]{:S(2)}) collective-permute-start(f32[1,16,16]{2,1,0:T(8,128)S(1)} %reshape.169), channel_id=1, source_target_pairs={{0,1},{1,2},{2,3},{3,4},{4,5},{5,6},{6,7},{7,8},{8,9},{9,10},{10,1... | collective-permute-start | bytes 3080 | tf_op jit(solution)/shard_map/ppermute | solution.py:17
  7.1 17.1 %collective-permute-start = (f32[1,16,16]{2,1,0:T(8,128)S(1)}, f32[1,16,16]{2,1,0:T(8,128)S(1)}, u32[]{:S(2)}, u32[]{:S(2)}) collective-permute-start(f32[1,16,16]{2,1,0:T(8,128)S(1)} %reshape.169), channel_id=1, source_target_pairs={{1,0},{2,1},{3,2},{4,3},{5,4},{6,5},{7,6},{8,7},{9,8},{10,9},{11,1... | collective-permute-start | bytes 3080 | tf_op jit(solution)/shard_map/ppermute | solution.py:20
  13.5 10.7 %all-to-all-start = ((f32[4,1,256]{2,1,0:T(1,128)}), f32[4,1,256]{2,1,0:T(1,128)S(1)}, u32[]{:S(2)}, u32[]{:S(2)}) async-start(f32[4,1,256]{2,1,0:T(1,128)} %stack.18), calls=%async_computation | async-start | bytes 8192 | tf_op jit(solution)/shard_map/all_to_all | solution.py:67
  16.8 6.1 %copy-start.4 = (u32[256]{0:T(256)S(1)}, u32[256]{0:T(256)}, u32[]{:S(2)}) copy-start(u32[256]{0:T(256)} %constant.53) | copy-start | bytes 3076
  22.1 5.1 %copy-start.3 = (s32[8,1024]{1,0:T(8,128)S(1)}, s32[8,1024]{1,0:T(8,128)}, u32[]{:S(2)}) copy-start(s32[8,1024]{1,0:T(8,128)} %param.7) | copy-start | bytes 98308
  22.1 111.8 %copy-start.2 = (f32[32,64,64]{2,1,0:T(8,128)S(1)}, f32[32,64,64]{2,1,0:T(8,128)}, u32[]{:S(2)}) copy-start(f32[32,64,64]{2,1,0:T(8,128)} %param.9) | copy-start | bytes 1572868
  117.5 12.0 %collective-permute-start.3 = (f32[1,16,16]{2,1,0:T(8,128)S(1)}, f32[1,16,16]{2,1,0:T(8,128)S(1)}, u32[]{:S(2)}, u32[]{:S(2)}) collective-permute-start(f32[1,16,16]{2,1,0:T(8,128)S(1)} %fusion.45), channel_id=1, source_target_pairs={{0,1},{1,2},{2,3},{3,4},{4,5},{5,6},{6,7},{7,8},{8,9},{9,10},{10,1... | collective-permute-start | bytes 3080 | tf_op jit(solution)/shard_map/ppermute | solution.py:17
  121.2 8.3 %collective-permute-start.2 = (f32[1,16,16]{2,1,0:T(8,128)S(1)}, f32[1,16,16]{2,1,0:T(8,128)S(1)}, u32[]{:S(2)}, u32[]{:S(2)}) collective-permute-start(f32[1,16,16]{2,1,0:T(8,128)S(1)} %fusion.45), channel_id=1, source_target_pairs={{1,0},{2,1},{3,2},{4,3},{5,4},{6,5},{7,6},{8,7},{9,8},{10,9},{11,1... | collective-permute-start | bytes 3080 | tf_op jit(solution)/shard_map/ppermute | solution.py:20
  126.2 7.6 %all-to-all-start.1 = ((f32[4,1,256]{2,1,0:T(1,128)}), f32[4,1,256]{2,1,0:T(1,128)S(1)}, u32[]{:S(2)}, u32[]{:S(2)}) async-start(f32[4,1,256]{2,1,0:T(1,128)} %stack.20), calls=%async_computation.1 | async-start | bytes 8192 | tf_op jit(solution)/shard_map/all_to_all | solution.py:67
  137.8 1.3 copy-start.1
  227.1 16.4 %collective-permute-start.5 = (f32[1,16,16]{2,1,0:T(8,128)S(1)}, f32[1,16,16]{2,1,0:T(8,128)S(1)}, u32[]{:S(2)}, u32[]{:S(2)}) collective-permute-start(f32[1,16,16]{2,1,0:T(8,128)S(1)} %fusion.40), channel_id=1, source_target_pairs={{0,1},{1,2},{2,3},{3,4},{4,5},{5,6},{6,7},{7,8},{8,9},{9,10},{10,1... | collective-permute-start | bytes 3080 | tf_op jit(solution)/shard_map/ppermute | solution.py:17
  229.7 13.7 %collective-permute-start.4 = (f32[1,16,16]{2,1,0:T(8,128)S(1)}, f32[1,16,16]{2,1,0:T(8,128)S(1)}, u32[]{:S(2)}, u32[]{:S(2)}) collective-permute-start(f32[1,16,16]{2,1,0:T(8,128)S(1)} %fusion.40), channel_id=1, source_target_pairs={{1,0},{2,1},{3,2},{4,3},{5,4},{6,5},{7,6},{8,7},{9,8},{10,9},{11,1... | collective-permute-start | bytes 3080 | tf_op jit(solution)/shard_map/ppermute | solution.py:20
  240.2 7.7 %all-to-all-start.2 = ((f32[4,1,256]{2,1,0:T(1,128)}), f32[4,1,256]{2,1,0:T(1,128)S(1)}, u32[]{:S(2)}, u32[]{:S(2)}) async-start(f32[4,1,256]{2,1,0:T(1,128)} %stack.22), calls=%async_computation.2 | async-start | bytes 8192 | tf_op jit(solution)/shard_map/all_to_all | solution.py:67
  336.9 11.3 %collective-permute-start.7 = (f32[1,16,16]{2,1,0:T(8,128)S(1)}, f32[1,16,16]{2,1,0:T(8,128)S(1)}, u32[]{:S(2)}, u32[]{:S(2)}) collective-permute-start(f32[1,16,16]{2,1,0:T(8,128)S(1)} %fusion.35), channel_id=1, source_target_pairs={{0,1},{1,2},{2,3},{3,4},{4,5},{5,6},{6,7},{7,8},{8,9},{9,10},{10,1... | collective-permute-start | bytes 3080 | tf_op jit(solution)/shard_map/ppermute | solution.py:17
  340.6 7.7 %collective-permute-start.6 = (f32[1,16,16]{2,1,0:T(8,128)S(1)}, f32[1,16,16]{2,1,0:T(8,128)S(1)}, u32[]{:S(2)}, u32[]{:S(2)}) collective-permute-start(f32[1,16,16]{2,1,0:T(8,128)S(1)} %fusion.35), channel_id=1, source_target_pairs={{1,0},{2,1},{3,2},{4,3},{5,4},{6,5},{7,6},{8,7},{9,8},{10,9},{11,1... | collective-permute-start | bytes 3080 | tf_op jit(solution)/shard_map/ppermute | solution.py:20
  345.0 7.7 %all-to-all-start.3 = ((f32[4,1,256]{2,1,0:T(1,128)}), f32[4,1,256]{2,1,0:T(1,128)S(1)}, u32[]{:S(2)}, u32[]{:S(2)}) async-start(f32[4,1,256]{2,1,0:T(1,128)} %stack.24), calls=%async_computation.3 | async-start | bytes 8192 | tf_op jit(solution)/shard_map/all_to_all | solution.py:67
